TPU v7x, 512 devices: a whole 4x8x8 slice. The times are simulated.
512 devices in a mesh: pipe: 32 (over z, y_hi), expert: 16 (over y_lo, x, core).
Axes of the slice: x: 4, y: 8 (y_hi: 4, y_lo: 2; y = y_hi * 2 + y_lo), z: 8, core: 2. Of those that a mesh axis runs over, the one named last changes fastest.
Arguments:
- tokens: bfloat16 [65536, 2048], P(('pipe', 'expert')), may hold values from -6 to 6
- cotangent: bfloat16 [65536, 2048], P(('pipe', 'expert')), may hold values from -6 to 6
- chosen: int32 [512, 64, 2], P(('pipe', 'expert')), may hold values from 0 to 127, as said below
- gate_value: bfloat16 [512, 64, 2], P(('pipe', 'expert')), may hold values from 0.049804688 to 1
- gate_weight: bfloat16 [2048, 65536], P(None, ('pipe', 'expert')), may hold values from -0.125 to 0.125
- up_weight: bfloat16 [2048, 65536], P(None, ('pipe', 'expert')), may hold values from -0.125 to 0.125
- down_weight: bfloat16 [65536, 2048], P(('pipe', 'expert')), may hold values from -0.1875 to 0.1875
Outputs:
- token_grad: bfloat16 [65536, 2048], P(('pipe', 'expert'))
- gate_grad: float32 [512, 64, 2], P(('pipe', 'expert'))
- gate_weight_grad: bfloat16 [2048, 65536], P(None, ('pipe', 'expert'))
- up_weight_grad: bfloat16 [2048, 65536], P(None, ('pipe', 'expert'))
- down_weight_grad: bfloat16 [65536, 2048], P(('pipe', 'expert'))
Inputs may be any that keep to these rules, and one draw needn't show every extreme that they name: `chosen`: for each routing group and expert, the 2 entries are different token indices within that group's 128 tokens.
All inputs are finite; a program needn't handle non-finite values.
Results may differ from a plain program's by a relative error of at most 0.0095.
Values may be sent and summed in bfloat16 or wider, within the bound.
No kernel may reach another device: no remote copies, remote signals or barrier semaphores. Data moves between devices by JAX's collectives and lax.ppermute only.
A program may use at most 128 MiB of HBM per device.

v0:
```python
import jax
import jax.numpy as jnp
from jax import lax
from jax.sharding import PartitionSpec as P


def select_rows(tokens, cotangent, list_flat):
    picked = jnp.take(tokens, list_flat, axis=0)
    dpicked = jnp.take(cotangent, list_flat, axis=0)
    return (picked, dpicked)


def expert_work(rows_x, rows_dy, rows_gate, gate_weight, up_weight, down_weight):
    feature_width = rows_x.shape[-1]
    picked = rows_x.reshape(-1, feature_width)
    dpicked = rows_dy.reshape(-1, feature_width)
    factor = rows_gate.reshape(-1).astype(jnp.float32)[:, None]
    contract_rows = (((0,), (0,)), ((), ()))
    contract_units = (((1,), (1,)), ((), ()))
    gate_pre = jnp.dot(picked, gate_weight, preferred_element_type=jnp.float32)
    up_pre = jnp.dot(picked, up_weight, preferred_element_type=jnp.float32)
    back = lax.dot_general(dpicked, down_weight, contract_units, preferred_element_type=jnp.float32)
    logistic = jax.nn.sigmoid(gate_pre)
    activated = gate_pre * logistic
    hidden = (activated * up_pre).astype(jnp.bfloat16)
    router = jnp.sum(hidden.astype(jnp.float32) * back, axis=1)
    hidden_grad = factor * back
    gate_pre_grad = (hidden_grad * up_pre * logistic * (1.0 + gate_pre * (1.0 - logistic))).astype(
        jnp.bfloat16
    )
    up_pre_grad = (hidden_grad * activated).astype(jnp.bfloat16)
    scaled = (factor * dpicked.astype(jnp.float32)).astype(jnp.bfloat16)
    down_grad = lax.dot_general(
        hidden, scaled, contract_rows, preferred_element_type=jnp.float32
    ).astype(jnp.bfloat16)
    gate_grad_w = lax.dot_general(
        picked, gate_pre_grad, contract_rows, preferred_element_type=jnp.float32
    ).astype(jnp.bfloat16)
    up_grad_w = lax.dot_general(
        picked, up_pre_grad, contract_rows, preferred_element_type=jnp.float32
    ).astype(jnp.bfloat16)
    block_grad = lax.dot_general(
        gate_pre_grad, gate_weight, contract_units, preferred_element_type=jnp.float32
    )
    block_grad = block_grad + lax.dot_general(
        up_pre_grad, up_weight, contract_units, preferred_element_type=jnp.float32
    )
    return (block_grad.astype(jnp.bfloat16), router, gate_grad_w, up_grad_w, down_grad)


def per_device(tokens, cotangent, chosen, gate_value, gate_weight, up_weight, down_weight):
    column_count = lax.axis_size("expert")
    pipe_count = lax.axis_size("pipe")
    block_count = min(8, column_count)
    per_pipe = column_count // block_count
    pick_count = chosen.shape[2]
    feature_width = tokens.shape[1]
    my_column = lax.axis_index("expert")
    list_flat = chosen[0].reshape(-1)
    picked, dpicked = select_rows(tokens, cotangent, list_flat)
    sent_x = picked.reshape(pipe_count, per_pipe, pick_count, feature_width)
    sent_dy = dpicked.reshape(pipe_count, per_pipe, pick_count, feature_width)
    sent_gate = gate_value[0].reshape(pipe_count, per_pipe, pick_count)
    got_x, got_dy, got_gate = (
        lax.all_to_all(sent_x, "pipe", split_axis=0, concat_axis=0, tiled=True),
        lax.all_to_all(sent_dy, "pipe", split_axis=0, concat_axis=0, tiled=True),
        lax.all_to_all(sent_gate, "pipe", split_axis=0, concat_axis=0, tiled=True),
    )
    wide_x = jnp.repeat(got_x, block_count, axis=1)
    wide_dy = jnp.repeat(got_dy, block_count, axis=1)
    wide_gate = jnp.repeat(got_gate, block_count, axis=1)
    rows_x, rows_dy, rows_gate = (
        lax.all_to_all(wide_x, "expert", split_axis=1, concat_axis=1, tiled=True),
        lax.all_to_all(wide_dy, "expert", split_axis=1, concat_axis=1, tiled=True),
        lax.all_to_all(wide_gate, "expert", split_axis=1, concat_axis=1, tiled=True),
    )
    block_grad, router, gate_weight_grad, up_weight_grad, down_weight_grad = expert_work(
        rows_x, rows_dy, rows_gate, gate_weight, up_weight, down_weight
    )
    my_expert = my_column // block_count
    router_grid = router.reshape(1, pipe_count, column_count, pick_count)
    expert_slots = jnp.arange(per_pipe, dtype=jnp.int32)[:, None, None, None]
    placed_router = jnp.where(expert_slots == my_expert, router_grid, jnp.float32(0.0))
    router_totals = lax.psum(placed_router, "expert")
    router_mine = lax.dynamic_index_in_dim(router_totals, my_column, axis=2, keepdims=False)
    router_home = jnp.transpose(router_mine, (1, 0, 2))
    returned = lax.all_to_all(
        block_grad.reshape(pipe_count, column_count, pick_count, feature_width),
        "expert",
        split_axis=1,
        concat_axis=1,
        tiled=True,
    )
    summed = jnp.sum(
        returned.astype(jnp.float32).reshape(
            pipe_count, per_pipe, block_count, pick_count, feature_width
        ),
        axis=2,
    )
    home_rows, home_router = (
        lax.all_to_all(summed, "pipe", split_axis=0, concat_axis=0, tiled=True),
        lax.all_to_all(router_home, "pipe", split_axis=0, concat_axis=0, tiled=True),
    )
    flat_rows = home_rows.reshape(-1, feature_width)
    columns = jnp.arange(tokens.shape[0], dtype=jnp.int32)
    onehot = (list_flat[:, None] == columns[None, :]).astype(jnp.float32)
    token_grad = lax.dot_general(
        onehot,
        flat_rows,
        (((0,), (0,)), ((), ())),
        precision=lax.Precision.HIGHEST,
        preferred_element_type=jnp.float32,
    ).astype(jnp.bfloat16)
    gate_grad = home_router.reshape(1, -1, pick_count)
    return (token_grad, gate_grad, gate_weight_grad, up_weight_grad, down_weight_grad)


def solution(mesh):
    return jax.shard_map(
        per_device,
        mesh=mesh,
        in_specs=(
            P(("pipe", "expert"), None),
            P(("pipe", "expert"), None),
            P(("pipe", "expert"), None, None),
            P(("pipe", "expert"), None, None),
            P(None, ("pipe", "expert")),
            P(None, ("pipe", "expert")),
            P(("pipe", "expert"), None),
        ),
        out_specs=(
            P(("pipe", "expert"), None),
            P(("pipe", "expert"), None, None),
            P(None, ("pipe", "expert")),
            P(None, ("pipe", "expert")),
            P(("pipe", "expert"), None),
        ),
        check_vma=False,
    )
```

profile of v0, /device:TPU:87, one launch (start us, length us, event | category | flops | bytes accessed | tf_op | source)
XLA Modules:
  0.0 450.7 jit_solution(946452296318267621)
XLA Ops:
  0.6 0.0 copy-start
  0.6 0.0 copy-start.4
  0.7 0.9 reshape_squeeze.4
  1.5 0.6 copy.80
  2.1 14.6 %all-to-all-start = ((bf16[32,2,2]{1,2,0:T(2,128)(2,1)}), bf16[32,2,2]{1,2,0:T(2,128)(2,1)S(1)}, u32[]{:S(2)}, u32[]{:S(2)}) async-start(bf16[32,2,2]{1,2,0:T(2,128)(2,1)} %copy.80), calls=%async_computation | async-start | bytes 32768 | tf_op jit(solution)/shard_map/all_to_all | solution.py:67
  16.7 0.8 copy.79
  17.5 0.1 eq.26
  17.7 2.6 gather_fusion.1
  20.3 0.9 gather_fusion
  21.2 3.8 all-to-all-done
  25.0 0.1 copy.81
  25.1 0.6 broadcast_in_dim.43
  25.7 6.7 %all-to-all-start.1 = ((bf16[32,16,2]{0,2,1:T(2,128)(2,1)}), bf16[32,16,2]{0,2,1:T(2,128)(2,1)S(1)}, u32[]{:S(2)}, u32[]{:S(2)}) async-start(bf16[32,16,2]{0,2,1:T(2,128)(2,1)} %bitcast), calls=%async_computation.1 | async-start | bytes 16384 | tf_op jit(solution)/shard_map/all_to_all | solution.py:75
  32.4 0.2 broadcast_select_fusion.1
  32.5 1.1 reshape.71
  33.7 2.5 all-to-all-done.1
  36.2 6.9 %all-to-all-start.4 = ((bf16[32,2,2,2048]{3,2,1,0:T(2,128)(2,1)}), bf16[32,2,2,2048]{3,2,1,0:T(2,128)(2,1)S(1)}, u32[]{:S(2)}, u32[]{:S(2)}) async-start(bf16[32,2,2,2048]{3,2,1,0:T(2,128)(2,1)} %reshape.71), calls=%async_computation.4 | async-start | bytes 1048576 | tf_op jit(solution)/shard_map/all_to_all | solution.py:65
  43.1 1.1 reshape.68
  44.2 18.4 %all-to-all-done.4 = bf16[32,2,2,2048]{3,2,1,0:T(2,128)(2,1)S(1)} async-done(((bf16[32,2,2,2048]{3,2,1,0:T(2,128)(2,1)}), bf16[32,2,2,2048]{3,2,1,0:T(2,128)(2,1)S(1)}, u32[]{:S(2)}, u32[]{:S(2)}) %all-to-all-start.4) | async-done | bytes 524320 | tf_op jit(solution)/shard_map/all_to_all | solution.py:65
  62.6 6.6 %all-to-all-start.2 = ((bf16[32,2,2,2048]{3,2,1,0:T(2,128)(2,1)}), bf16[32,2,2,2048]{3,2,1,0:T(2,128)(2,1)S(1)}, u32[]{:S(2)}, u32[]{:S(2)}) async-start(bf16[32,2,2,2048]{3,2,1,0:T(2,128)(2,1)} %reshape.68), calls=%async_computation.2 | async-start | bytes 1048576 | tf_op jit(solution)/shard_map/all_to_all | solution.py:66
  69.2 0.4 copy.86
  69.5 17.4 %all-to-all-done.2 = bf16[32,2,2,2048]{3,2,1,0:T(2,128)(2,1)S(1)} async-done(((bf16[32,2,2,2048]{3,2,1,0:T(2,128)(2,1)}), bf16[32,2,2,2048]{3,2,1,0:T(2,128)(2,1)S(1)}, u32[]{:S(2)}, u32[]{:S(2)}) %all-to-all-start.2) | async-done | bytes 524320 | tf_op jit(solution)/shard_map/all_to_all | solution.py:66
  87.0 5.5 %broadcast_in_dim.45 = bf16[32,2,8,2,2048]{4,3,0,2,1:T(2,128)(2,1)} broadcast(bf16[32,2,2,2048]{3,2,0,1:T(2,128)(2,1)S(1)} %copy.86), dimensions={0,1,3,4} | broadcast | bytes 4718592 | tf_op jit(solution)/shard_map/broadcast_in_dim | solution.py:69
  92.5 7.1 %all-to-all-start.5 = ((bf16[32,16,2,2048]{3,2,0,1:T(2,128)(2,1)}), bf16[32,16,2,2048]{3,2,0,1:T(2,128)(2,1)}, u32[]{:S(2)}, u32[]{:S(2)}) async-start(bf16[32,16,2,2048]{3,2,0,1:T(2,128)(2,1)} %bitcast.30), calls=%async_computation.5 | async-start | bytes 8388608 | tf_op jit(solution)/shard_map/all_to_all | solution.py:73
  99.6 0.4 copy.84
  100.0 61.0 %all-to-all-done.5 = bf16[32,16,2,2048]{3,2,0,1:T(2,128)(2,1)} async-done(((bf16[32,16,2,2048]{3,2,0,1:T(2,128)(2,1)}), bf16[32,16,2,2048]{3,2,0,1:T(2,128)(2,1)}, u32[]{:S(2)}, u32[]{:S(2)}) %all-to-all-start.5) | async-done | bytes 4194336 | tf_op jit(solution)/shard_map/all_to_all | solution.py:73
  160.9 5.5 %broadcast_in_dim.44 = bf16[32,2,8,2,2048]{4,3,0,2,1:T(2,128)(2,1)} broadcast(bf16[32,2,2,2048]{3,2,0,1:T(2,128)(2,1)S(1)} %copy.84), dimensions={0,1,3,4} | broadcast | bytes 4718592 | tf_op jit(solution)/shard_map/broadcast_in_dim | solution.py:70
  166.4 5.9 %all-to-all-start.3 = ((bf16[32,16,2,2048]{3,2,0,1:T(2,128)(2,1)}), bf16[32,16,2,2048]{3,2,0,1:T(2,128)(2,1)}, u32[]{:S(2)}, u32[]{:S(2)}) async-start(bf16[32,16,2,2048]{3,2,0,1:T(2,128)(2,1)} %bitcast.29), calls=%async_computation.3 | async-start | bytes 8388608 | tf_op jit(solution)/shard_map/all_to_all | solution.py:74
  172.3 0.2 copy.83
  172.5 0.2 reshape.79
  172.7 8.6 %copy.87 = bf16[32,16,2,2048]{3,2,1,0:T(2,128)(2,1)} copy(bf16[32,16,2,2048]{3,2,0,1:T(2,128)(2,1)} %all-to-all-done.5) | data formatting | bytes 8388608 | tf_op jit(solution)/shard_map/all_to_all | solution.py:73
  181.4 7.2 %reshape.73 = bf16[1024,2048]{1,0:T(8,128)(2,1)} reshape(bf16[32,16,2,2048]{3,2,1,0:T(2,128)(2,1)} %copy.87) | data formatting | bytes 8388608 | tf_op jit(solution)/shard_map/reshape | solution.py:15
  188.6 3.9 fusion.6
  192.4 1.5 fusion.5
  194.0 39.6 %all-to-all-done.3 = bf16[32,16,2,2048]{3,2,0,1:T(2,128)(2,1)} async-done(((bf16[32,16,2,2048]{3,2,0,1:T(2,128)(2,1)}), bf16[32,16,2,2048]{3,2,0,1:T(2,128)(2,1)}, u32[]{:S(2)}, u32[]{:S(2)}) %all-to-all-start.3) | async-done | bytes 4194336 | tf_op jit(solution)/shard_map/all_to_all | solution.py:74
  233.6 8.7 %copy.85 = bf16[32,16,2,2048]{3,2,1,0:T(2,128)(2,1)} copy(bf16[32,16,2,2048]{3,2,0,1:T(2,128)(2,1)} %all-to-all-done.3) | data formatting | bytes 8388608 | tf_op jit(solution)/shard_map/all_to_all | solution.py:74
  242.3 7.5 %reshape.70 = bf16[1024,2048]{1,0:T(8,128)(2,1)} reshape(bf16[32,16,2,2048]{3,2,1,0:T(2,128)(2,1)} %copy.85) | data formatting | bytes 8388608 | tf_op jit(solution)/shard_map/reshape | solution.py:16
  249.7 3.9 multiply_reduce_fusion
  253.6 1.3 fusion.7
  254.9 3.2 add_convert_fusion
  258.1 7.7 %reshape.74 = bf16[32,16,2,2048]{3,2,1,0:T(2,128)(2,1)} reshape(bf16[1024,2048]{1,0:T(8,128)(2,1)} %add_convert_fusion) | data formatting | bytes 8388608 | tf_op jit(solution)/shard_map/reshape | solution.py:88
  265.8 8.0 %copy.88 = bf16[32,16,2,2048]{3,2,0,1:T(2,128)(2,1)} copy(bf16[32,16,2,2048]{3,2,1,0:T(2,128)(2,1)} %reshape.74) | data formatting | bytes 8388608 | tf_op jit(solution)/shard_map/reshape | solution.py:88
  273.8 5.9 %all-to-all-start.6 = ((bf16[32,16,2,2048]{3,2,0,1:T(2,128)(2,1)}), bf16[32,16,2,2048]{3,2,0,1:T(2,128)(2,1)}, u32[]{:S(2)}, u32[]{:S(2)}) async-start(bf16[32,16,2,2048]{3,2,0,1:T(2,128)(2,1)} %copy.88), calls=%async_computation.6 | async-start | bytes 8388608 | tf_op jit(solution)/shard_map/all_to_all | solution.py:87
  279.7 0.2 broadcast_in_dim.47
  279.9 0.2 copy.90
  280.1 0.1 broadcast_select_fusion.2
  280.2 101.7 %psum.7 = f32[2,32,16,2]{1,3,2,0:T(2,128)S(1)} all-reduce(f32[2,32,16,2]{1,3,2,0:T(2,128)S(1)} %broadcast_select_fusion.2), channel_id=1, replica_groups=mesh['pipe'=32,'expert'=16] {'expert'}, use_global_device_ids=true, to_apply=%region_2.4 | all-reduce | flops 2048 | bytes 16384 | tf_op jit(solution)/shard_map/psum | solution.py:84
  381.9 0.7 copy.91
  382.7 0.0 all-to-all-done.6
  382.7 6.6 %all-to-all-start.8 = ((f32[32,2,2]{2,1,0:T(2,128)}), f32[32,2,2]{2,1,0:T(2,128)S(1)}, u32[]{:S(2)}, u32[]{:S(2)}) async-start(f32[32,2,2]{2,1,0:T(2,128)} %copy.91), calls=%async_computation.8 | async-start | bytes 65536 | tf_op jit(solution)/shard_map/all_to_all | solution.py:102
  389.2 6.3 %convert_reduce_fusion = f32[32,2,2,2048]{3,2,0,1:T(2,128)S(1)} fusion(bf16[32,16,2,2048]{3,2,0,1:T(2,128)(2,1)} %all-to-all-done.6), kind=kLoop, calls=%fused_computation.2 | loop fusion | flops 3932160 | bytes 5242880 | tf_op jit(solution)/shard_map/reduce_sum | solution.py:94
  395.6 1.1 copy.89
  396.7 0.9 all-to-all-done.8
  397.6 10.8 %all-to-all-start.7 = ((f32[32,2,2,2048]{3,2,1,0:T(2,128)}), f32[32,2,2,2048]{3,2,1,0:T(2,128)S(1)}, u32[]{:S(2)}, u32[]{:S(2)}) async-start(f32[32,2,2,2048]{3,2,1,0:T(2,128)} %copy.89), calls=%async_computation.7 | async-start | bytes 2097152 | tf_op jit(solution)/shard_map/all_to_all | solution.py:101
  408.3 0.0 copy-start.3
  408.3 0.0 copy-start.5
  408.4 4.4 convolution_convert_fusion.1
  412.8 0.0 copy-done.3
  412.8 2.1 convolution_convert_fusion
  414.9 1.9 fusion.2
  416.8 0.6 copy.93
  417.4 30.8 %all-to-all-done.7 = f32[32,2,2,2048]{3,2,1,0:T(2,128)S(1)} async-done(((f32[32,2,2,2048]{3,2,1,0:T(2,128)}), f32[32,2,2,2048]{3,2,1,0:T(2,128)S(1)}, u32[]{:S(2)}, u32[]{:S(2)}) %all-to-all-start.7) | async-done | bytes 1048608 | tf_op jit(solution)/shard_map/all_to_all | solution.py:101
  448.2 0.7 reshape.77
  449.0 1.5 convolution_convert_fusion.2
  (17 shorter events, 0.1 us)
Async XLA Ops:
  0.6 187.9 %copy-start = (bf16[2048,128]{1,0:T(8,128)(2,1)S(1)}, bf16[2048,128]{1,0:T(8,128)(2,1)}, u32[]{:S(2)}) copy-start(bf16[2048,128]{1,0:T(8,128)(2,1)} %param.13) | copy-start | bytes 1572868
  0.6 19.6 %copy-start.4 = (bf16[128,2048]{1,0:T(8,128)(2,1)S(1)}, bf16[128,2048]{1,0:T(8,128)(2,1)}, u32[]{:S(2)}) copy-start(bf16[128,2048]{1,0:T(8,128)(2,1)} %param.10) | copy-start | bytes 1572868
  2.1 22.9 %all-to-all-start = ((bf16[32,2,2]{1,2,0:T(2,128)(2,1)}), bf16[32,2,2]{1,2,0:T(2,128)(2,1)S(1)}, u32[]{:S(2)}, u32[]{:S(2)}) async-start(bf16[32,2,2]{1,2,0:T(2,128)(2,1)} %copy.80), calls=%async_computation | async-start | bytes 32768 | tf_op jit(solution)/shard_map/all_to_all | solution.py:67
  25.7 10.4 %all-to-all-start.1 = ((bf16[32,16,2]{0,2,1:T(2,128)(2,1)}), bf16[32,16,2]{0,2,1:T(2,128)(2,1)S(1)}, u32[]{:S(2)}, u32[]{:S(2)}) async-start(bf16[32,16,2]{0,2,1:T(2,128)(2,1)} %bitcast), calls=%async_computation.1 | async-start | bytes 16384 | tf_op jit(solution)/shard_map/all_to_all | solution.py:75
  36.2 26.4 %all-to-all-start.4 = ((bf16[32,2,2,2048]{3,2,1,0:T(2,128)(2,1)}), bf16[32,2,2,2048]{3,2,1,0:T(2,128)(2,1)S(1)}, u32[]{:S(2)}, u32[]{:S(2)}) async-start(bf16[32,2,2,2048]{3,2,1,0:T(2,128)(2,1)} %reshape.71), calls=%async_computation.4 | async-start | bytes 1048576 | tf_op jit(solution)/shard_map/all_to_all | solution.py:65
  62.6 24.4 %all-to-all-start.2 = ((bf16[32,2,2,2048]{3,2,1,0:T(2,128)(2,1)}), bf16[32,2,2,2048]{3,2,1,0:T(2,128)(2,1)S(1)}, u32[]{:S(2)}, u32[]{:S(2)}) async-start(bf16[32,2,2,2048]{3,2,1,0:T(2,128)(2,1)} %reshape.68), calls=%async_computation.2 | async-start | bytes 1048576 | tf_op jit(solution)/shard_map/all_to_all | solution.py:66
  92.5 68.5 %all-to-all-start.5 = ((bf16[32,16,2,2048]{3,2,0,1:T(2,128)(2,1)}), bf16[32,16,2,2048]{3,2,0,1:T(2,128)(2,1)}, u32[]{:S(2)}, u32[]{:S(2)}) async-start(bf16[32,16,2,2048]{3,2,0,1:T(2,128)(2,1)} %bitcast.30), calls=%async_computation.5 | async-start | bytes 8388608 | tf_op jit(solution)/shard_map/all_to_all | solution.py:73
  166.4 67.1 %all-to-all-start.3 = ((bf16[32,16,2,2048]{3,2,0,1:T(2,128)(2,1)}), bf16[32,16,2,2048]{3,2,0,1:T(2,128)(2,1)}, u32[]{:S(2)}, u32[]{:S(2)}) async-start(bf16[32,16,2,2048]{3,2,0,1:T(2,128)(2,1)} %bitcast.29), calls=%async_computation.3 | async-start | bytes 8388608 | tf_op jit(solution)/shard_map/all_to_all | solution.py:74
  188.6 3.9 copy-start.2
  188.6 3.9 copy-start.6
  242.3 7.5 %copy-start.7 = (bf16[128,2048]{1,0:T(8,128)(2,1)S(1)}, bf16[128,2048]{1,0:T(8,128)(2,1)}, u32[]{:S(2)}) copy-start(bf16[128,2048]{1,0:T(8,128)(2,1)} %param.15) | copy-start | bytes 1572868
  273.8 108.9 %all-to-all-start.6 = ((bf16[32,16,2,2048]{3,2,0,1:T(2,128)(2,1)}), bf16[32,16,2,2048]{3,2,0,1:T(2,128)(2,1)}, u32[]{:S(2)}, u32[]{:S(2)}) async-start(bf16[32,16,2,2048]{3,2,0,1:T(2,128)(2,1)} %copy.88), calls=%async_computation.6 | async-start | bytes 8388608 | tf_op jit(solution)/shard_map/all_to_all | solution.py:87
  382.7 14.9 %all-to-all-start.8 = ((f32[32,2,2]{2,1,0:T(2,128)}), f32[32,2,2]{2,1,0:T(2,128)S(1)}, u32[]{:S(2)}, u32[]{:S(2)}) async-start(f32[32,2,2]{2,1,0:T(2,128)} %copy.91), calls=%async_computation.8 | async-start | bytes 65536 | tf_op jit(solution)/shard_map/all_to_all | solution.py:102
  397.6 50.7 %all-to-all-start.7 = ((f32[32,2,2,2048]{3,2,1,0:T(2,128)}), f32[32,2,2,2048]{3,2,1,0:T(2,128)S(1)}, u32[]{:S(2)}, u32[]{:S(2)}) async-start(f32[32,2,2,2048]{3,2,1,0:T(2,128)} %copy.89), calls=%async_computation.7 | async-start | bytes 2097152 | tf_op jit(solution)/shard_map/all_to_all | solution.py:101
  408.3 4.5 copy-start.3
  408.3 6.6 %copy-start.5 = (bf16[1024,2048]{1,0:T(8,128)(2,1)S(1)}, bf16[1024,2048]{1,0:T(8,128)(2,1)}, u32[]{:S(2)}) copy-start(bf16[1024,2048]{1,0:T(8,128)(2,1)} %reshape.70) | copy-start | bytes 12582916
  414.9 35.6 %copy-start.1 = (bf16[2048,128]{1,0:T(8,128)(2,1)S(1)}, bf16[2048,128]{1,0:T(8,128)(2,1)}, u32[]{:S(2)}) copy-start(bf16[2048,128]{1,0:T(8,128)(2,1)} %param.13) | copy-start | bytes 1572868
where the time goes:
time: 459 us; the launch traced here: 451 us
  waiting for transfers between devices  174 us (38%)
  blocking collectives  102 us (22%)
  local copies, waits for them, and re-layouts  72.2 us (16%)
  starting transfers between devices  71.1 us (15%)
  matrix products  23.7 us (5%)
  other arithmetic  6.59 us (1%)
    psum x1, blocking collectives, per_device(): router_totals = lax.psum(placed_router, 'expert')  102 us
    all_to_all x1, waiting for transfers between devices, per_device(): lax.all_to_all(wide_x, 'expert', split_axis=1, concat_axis=1, tiled=True)  61 us
    all_to_all x1, waiting for transfers between devices, per_device(): lax.all_to_all(wide_dy, 'expert', split_axis=1, concat_axis=1, tiled=True)  39.6 us
    all_to_all x1, waiting for transfers between devices, per_device(): lax.all_to_all(summed, 'pipe', split_axis=0, concat_axis=0, tiled=True)  30.8 us
    all_to_all x1, waiting for transfers between devices, per_device(): lax.all_to_all(sent_x, 'pipe', split_axis=0, concat_axis=0, tiled=True)  18.4 us
    all_to_all x1, waiting for transfers between devices, per_device(): lax.all_to_all(sent_dy, 'pipe', split_axis=0, concat_axis=0, tiled=True)  17.4 us
    reshape x2, local copies, waits for them, and re-layouts, per_device(): block_grad.reshape(pipe_count, column_count, pick_count, feature_width)  15.7 us
    all_to_all x1, starting transfers between devices, per_device(): lax.all_to_all(sent_gate, 'pipe', split_axis=0, concat_axis=0, tiled=True)  14.6 us
  transfers between devices with their start and end apart: 9, of which 8 were waited for; matrix products, arithmetic and copies ran while one was open for 10% of the time, Pallas kernels for 0%

commit v1 on v0

--- a/solution.py
+++ b/solution.py
@@ -70,7 +70,12 @@
     wide_dy = jnp.repeat(got_dy, block_count, axis=1)
     wide_gate = jnp.repeat(got_gate, block_count, axis=1)
     rows_x, rows_dy, rows_gate = (
-        lax.all_to_all(wide_x, "expert", split_axis=1, concat_axis=1, tiled=True),
+        jnp.concatenate(
+            lax.all_to_all(
+                jnp.stack(jnp.split(wide_x, lax.axis_size("expert"), axis=1)), "expert", 0, 0
+            ),
+            axis=1,
+        ),
         lax.all_to_all(wide_dy, "expert", split_axis=1, concat_axis=1, tiled=True),
         lax.all_to_all(wide_gate, "expert", split_axis=1, concat_axis=1, tiled=True),
     )

time: 459 us -> 456 us (level)
  local copies, waits for them, and re-layouts: 72.2 us -> 84.2 us
  waiting for transfers between devices: 174 us -> 162 us
    all_to_all x1, waiting for transfers between devices: 61 us -> 45 us  [per_device(): lax.all_to_all(jnp.stack(jnp.split(wide_x, lax.axis_size('expert'), axis=...]
    unnamed x17 -> x32, local copies, waits for them, and re-layouts: 0.81 us -> 14.1 us
    all_to_all x1 -> x0, local copies, waits for them, and re-layouts: 8.64 us -> none  [per_device(): lax.all_to_all(wide_x, 'expert', split_axis=1, concat_axis=1, tiled=True)]
    another operation x0 -> x2, local copies, waits for them, and re-layouts: none -> 8.34 us  [the longest x1 7.46 us: expert_work(): picked = rows_x.reshape(-1, feature_width)]
  transfers between devices with their start and end apart: 9 -> 9, of which waited for: 8 -> 8; matrix products, arithmetic and copies ran while one was open for 10% -> 13% of each run, Pallas kernels for 0% -> 0%
where the time goes in v1:
time: 456 us; the launch traced here: 449 us
  waiting for transfers between devices  162 us (36%)
  blocking collectives  102 us (22%)
  local copies, waits for them, and re-layouts  84.2 us (18%)
  starting transfers between devices  71.6 us (16%)
  matrix products  21.6 us (5%)
  other arithmetic  6.59 us (1%)
    psum x1, blocking collectives, per_device(): router_totals = lax.psum(placed_router, 'expert')  102 us
    all_to_all x1, waiting for transfers between devices, per_device(): lax.all_to_all(jnp.stack(jnp.split(wide_x, lax.axis_size('expert'), axis=...  45 us
    all_to_all x1, waiting for transfers between devices, per_device(): lax.all_to_all(wide_dy, 'expert', split_axis=1, concat_axis=1, tiled=True)  43.4 us
    all_to_all x1, waiting for transfers between devices, per_device(): lax.all_to_all(summed, 'pipe', split_axis=0, concat_axis=0, tiled=True)  30.8 us
    all_to_all x1, waiting for transfers between devices, per_device(): lax.all_to_all(sent_dy, 'pipe', split_axis=0, concat_axis=0, tiled=True)  18.4 us
    all_to_all x1, waiting for transfers between devices, per_device(): lax.all_to_all(sent_x, 'pipe', split_axis=0, concat_axis=0, tiled=True)  17.4 us
    reshape x2, local copies, waits for them, and re-layouts, per_device(): block_grad.reshape(pipe_count, column_count, pick_count, feature_width)  15.7 us
    all_to_all x1, starting transfers between devices, per_device(): lax.all_to_all(sent_gate, 'pipe', split_axis=0, concat_axis=0, tiled=True)  14.6 us
  transfers between devices with their start and end apart: 9, of which 8 were waited for; matrix products, arithmetic and copies ran while one was open for 13% of the time, Pallas kernels for 0%

profile of v1, /device:TPU:87, one launch (start us, length us, event | category | flops | bytes accessed | tf_op | source)
XLA Modules:
  0.0 449.0 jit_solution(3630337077148495641)
XLA Ops:
  0.7 0.9 reshape_squeeze.4
  1.5 0.6 copy.112
  2.1 14.6 %all-to-all-start = ((bf16[32,2,2]{1,2,0:T(2,128)(2,1)}), bf16[32,2,2]{1,2,0:T(2,128)(2,1)S(1)}, u32[]{:S(2)}, u32[]{:S(2)}) async-start(bf16[32,2,2]{1,2,0:T(2,128)(2,1)} %copy.112), calls=%async_computation | async-start | bytes 32768 | tf_op jit(solution)/shard_map/all_to_all | solution.py:67
  16.7 0.8 copy.111
  17.7 2.6 gather_fusion.1
  20.3 0.9 gather_fusion
  21.2 3.8 all-to-all-done
  25.1 0.6 broadcast_in_dim.43
  25.7 6.7 %all-to-all-start.1 = ((bf16[32,16,2]{0,2,1:T(2,128)(2,1)}), bf16[32,16,2]{0,2,1:T(2,128)(2,1)S(1)}, u32[]{:S(2)}, u32[]{:S(2)}) async-start(bf16[32,16,2]{0,2,1:T(2,128)(2,1)} %bitcast), calls=%async_computation.1 | async-start | bytes 16384 | tf_op jit(solution)/shard_map/all_to_all | solution.py:80
  32.5 1.1 reshape.68
  33.7 2.5 all-to-all-done.1
  36.1 6.9 %all-to-all-start.2 = ((bf16[32,2,2,2048]{3,2,1,0:T(2,128)(2,1)}), bf16[32,2,2,2048]{3,2,1,0:T(2,128)(2,1)S(1)}, u32[]{:S(2)}, u32[]{:S(2)}) async-start(bf16[32,2,2,2048]{3,2,1,0:T(2,128)(2,1)} %reshape.68), calls=%async_computation.2 | async-start | bytes 1048576 | tf_op jit(solution)/shard_map/all_to_all | solution.py:66
  43.1 1.1 reshape.71
  44.2 18.4 %all-to-all-done.2 = bf16[32,2,2,2048]{3,2,1,0:T(2,128)(2,1)S(1)} async-done(((bf16[32,2,2,2048]{3,2,1,0:T(2,128)(2,1)}), bf16[32,2,2,2048]{3,2,1,0:T(2,128)(2,1)S(1)}, u32[]{:S(2)}, u32[]{:S(2)}) %all-to-all-start.2) | async-done | bytes 524320 | tf_op jit(solution)/shard_map/all_to_all | solution.py:66
  62.6 6.6 %all-to-all-start.4 = ((bf16[32,2,2,2048]{3,2,1,0:T(2,128)(2,1)}), bf16[32,2,2,2048]{3,2,1,0:T(2,128)(2,1)S(1)}, u32[]{:S(2)}, u32[]{:S(2)}) async-start(bf16[32,2,2,2048]{3,2,1,0:T(2,128)(2,1)} %reshape.71), calls=%async_computation.4 | async-start | bytes 1048576 | tf_op jit(solution)/shard_map/all_to_all | solution.py:65
  69.5 17.4 %all-to-all-done.4 = bf16[32,2,2,2048]{3,2,1,0:T(2,128)(2,1)S(1)} async-done(((bf16[32,2,2,2048]{3,2,1,0:T(2,128)(2,1)}), bf16[32,2,2,2048]{3,2,1,0:T(2,128)(2,1)S(1)}, u32[]{:S(2)}, u32[]{:S(2)}) %all-to-all-start.4) | async-done | bytes 524320 | tf_op jit(solution)/shard_map/all_to_all | solution.py:65
  87.0 5.5 %broadcast_in_dim.44 = bf16[32,2,8,2,2048]{4,3,0,2,1:T(2,128)(2,1)} broadcast(bf16[32,2,2,2048]{3,2,0,1:T(2,128)(2,1)S(1)} %copy.116), dimensions={0,1,3,4} | broadcast | bytes 4718592 | tf_op jit(solution)/shard_map/broadcast_in_dim | solution.py:70
  92.5 7.6 %all-to-all-start.3 = ((bf16[32,16,2,2048]{3,2,0,1:T(2,128)(2,1)}), bf16[32,16,2,2048]{3,2,0,1:T(2,128)(2,1)}, u32[]{:S(2)}, u32[]{:S(2)}) async-start(bf16[32,16,2,2048]{3,2,0,1:T(2,128)(2,1)} %bitcast.112), calls=%async_computation.3 | async-start | bytes 8388608 | tf_op jit(solution)/shard_map/all_to_all | solution.py:79
  100.4 3.2 broadcast_in_dim.45
  103.7 0.9 fusion.19
  104.6 0.9 fusion.18
  105.5 0.9 fusion.17
  106.4 0.9 fusion.16
  107.3 0.9 fusion.15
  108.1 0.9 fusion.14
  109.0 0.9 fusion.13
  109.9 0.9 fusion.12
  110.8 0.9 fusion.11
  111.6 0.9 fusion.10
  112.5 0.9 fusion.9
  113.4 0.9 fusion.8
  114.3 0.9 fusion.7
  115.2 0.9 fusion.6
  116.1 0.9 fusion.5
  117.0 0.9 fusion.4
  117.9 43.4 %all-to-all-done.3 = bf16[32,16,2,2048]{3,2,0,1:T(2,128)(2,1)} async-done(((bf16[32,16,2,2048]{3,2,0,1:T(2,128)(2,1)}), bf16[32,16,2,2048]{3,2,0,1:T(2,128)(2,1)}, u32[]{:S(2)}, u32[]{:S(2)}) %all-to-all-start.3) | async-done | bytes 4194336 | tf_op jit(solution)/shard_map/all_to_all | solution.py:79
  161.3 6.0 %all-to-all-start.5 = ((bf16[16,32,1,2,2048]{4,3,1,2,0:T(2,128)(2,1)}), bf16[16,32,1,2,2048]{4,3,1,2,0:T(2,128)(2,1)}, u32[]{:S(2)}, u32[]{:S(2)}) async-start(bf16[16,32,1,2,2048]{4,3,1,2,0:T(2,128)(2,1)} %fusion.4), calls=%async_computation.5 | async-start | bytes 8388608 | tf_op jit(solution)/shard_map/all_to_all | solution.py:74
  167.7 8.7 %copy.117 = bf16[32,16,2,2048]{3,2,1,0:T(2,128)(2,1)} copy(bf16[32,16,2,2048]{3,2,0,1:T(2,128)(2,1)} %all-to-all-done.3) | data formatting | bytes 8388608 | tf_op jit(solution)/shard_map/all_to_all | solution.py:79
  176.4 7.2 %reshape.70 = bf16[1024,2048]{1,0:T(8,128)(2,1)} reshape(bf16[32,16,2,2048]{3,2,1,0:T(2,128)(2,1)} %copy.117) | data formatting | bytes 8388608 | tf_op jit(solution)/shard_map/reshape | solution.py:16
  183.6 45.0 %all-to-all-done.5 = bf16[16,32,1,2,2048]{4,3,1,2,0:T(2,128)(2,1)} async-done(((bf16[16,32,1,2,2048]{4,3,1,2,0:T(2,128)(2,1)}), bf16[16,32,1,2,2048]{4,3,1,2,0:T(2,128)(2,1)}, u32[]{:S(2)}, u32[]{:S(2)}) %all-to-all-start.5) | async-done | bytes 4194336 | tf_op jit(solution)/shard_map/all_to_all | solution.py:74
  228.5 8.7 %copy.119 = bf16[32,16,1,2,2048]{4,3,1,0,2:T(2,128)(2,1)} copy(bf16[32,16,1,2,2048]{4,3,0,2,1:T(2,128)(2,1)} %bitcast.19) | data formatting | bytes 8388608 | tf_op jit(solution)/shard_map/reshape | solution.py:73
  237.2 7.5 %reshape_reshape.3 = bf16[1024,2048]{1,0:T(8,128)(2,1)} reshape(bf16[32,16,1,2,2048]{4,3,1,0,2:T(2,128)(2,1)} %copy.119) | data formatting | bytes 8388608 | tf_op jit(solution)/shard_map/reshape;reshape | solution.py:15
  244.7 3.9 fusion.22
  248.6 1.5 fusion.21
  250.2 1.7 multiply_reduce_fusion
  251.9 1.3 fusion.23
  253.2 3.2 add_convert_fusion
  256.4 7.7 %reshape.74 = bf16[32,16,2,2048]{3,2,1,0:T(2,128)(2,1)} reshape(bf16[1024,2048]{1,0:T(8,128)(2,1)} %add_convert_fusion) | data formatting | bytes 8388608 | tf_op jit(solution)/shard_map/reshape | solution.py:93
  264.1 8.0 %copy.120 = bf16[32,16,2,2048]{3,2,0,1:T(2,128)(2,1)} copy(bf16[32,16,2,2048]{3,2,1,0:T(2,128)(2,1)} %reshape.74) | data formatting | bytes 8388608 | tf_op jit(solution)/shard_map/reshape | solution.py:93
  272.1 5.9 %all-to-all-start.6 = ((bf16[32,16,2,2048]{3,2,0,1:T(2,128)(2,1)}), bf16[32,16,2,2048]{3,2,0,1:T(2,128)(2,1)}, u32[]{:S(2)}, u32[]{:S(2)}) async-start(bf16[32,16,2,2048]{3,2,0,1:T(2,128)(2,1)} %copy.120), calls=%async_computation.6 | async-start | bytes 8388608 | tf_op jit(solution)/shard_map/all_to_all | solution.py:92
  278.5 101.7 %psum.7 = f32[2,32,16,2]{1,3,2,0:T(2,128)S(1)} all-reduce(f32[2,32,16,2]{1,3,2,0:T(2,128)S(1)} %broadcast_select_fusion.2), channel_id=1, replica_groups=mesh['pipe'=32,'expert'=16] {'expert'}, use_global_device_ids=true, to_apply=%region_2.4 | all-reduce | flops 2048 | bytes 16384 | tf_op jit(solution)/shard_map/psum | solution.py:89
  380.2 0.7 copy.123
  380.9 6.6 %all-to-all-start.8 = ((f32[32,2,2]{2,1,0:T(2,128)}), f32[32,2,2]{2,1,0:T(2,128)S(1)}, u32[]{:S(2)}, u32[]{:S(2)}) async-start(f32[32,2,2]{2,1,0:T(2,128)} %copy.123), calls=%async_computation.8 | async-start | bytes 65536 | tf_op jit(solution)/shard_map/all_to_all | solution.py:107
  387.5 6.3 %convert_reduce_fusion = f32[32,2,2,2048]{3,2,0,1:T(2,128)S(1)} fusion(bf16[32,16,2,2048]{3,2,0,1:T(2,128)(2,1)} %all-to-all-done.6), kind=kLoop, calls=%fused_computation.2 | loop fusion | flops 3932160 | bytes 5242880 | tf_op jit(solution)/shard_map/reduce_sum | solution.py:99
  393.9 1.1 copy.121
  395.0 0.9 all-to-all-done.8
  395.8 10.8 %all-to-all-start.7 = ((f32[32,2,2,2048]{3,2,1,0:T(2,128)}), f32[32,2,2,2048]{3,2,1,0:T(2,128)S(1)}, u32[]{:S(2)}, u32[]{:S(2)}) async-start(f32[32,2,2,2048]{3,2,1,0:T(2,128)} %copy.121), calls=%async_computation.7 | async-start | bytes 2097152 | tf_op jit(solution)/shard_map/all_to_all | solution.py:106
  406.6 4.4 convolution_convert_fusion.1
  411.1 2.1 convolution_convert_fusion
  413.2 1.9 fusion.2
  415.1 0.6 copy.125
  415.7 30.8 %all-to-all-done.7 = f32[32,2,2,2048]{3,2,1,0:T(2,128)S(1)} async-done(((f32[32,2,2,2048]{3,2,1,0:T(2,128)}), f32[32,2,2,2048]{3,2,1,0:T(2,128)S(1)}, u32[]{:S(2)}, u32[]{:S(2)}) %all-to-all-start.7) | async-done | bytes 1048608 | tf_op jit(solution)/shard_map/all_to_all | solution.py:106
  446.5 0.7 reshape.77
  447.2 1.5 convolution_convert_fusion.2
  (33 shorter events, 2.0 us)
Async XLA Ops:
  0.6 244.1 %copy-start = (bf16[2048,128]{1,0:T(8,128)(2,1)S(1)}, bf16[2048,128]{1,0:T(8,128)(2,1)}, u32[]{:S(2)}) copy-start(bf16[2048,128]{1,0:T(8,128)(2,1)} %param.13) | copy-start | bytes 1572868
  0.6 19.6 %copy-start.3 = (bf16[128,2048]{1,0:T(8,128)(2,1)S(1)}, bf16[128,2048]{1,0:T(8,128)(2,1)}, u32[]{:S(2)}) copy-start(bf16[128,2048]{1,0:T(8,128)(2,1)} %param.10) | copy-start | bytes 1572868
  2.1 22.9 %all-to-all-start = ((bf16[32,2,2]{1,2,0:T(2,128)(2,1)}), bf16[32,2,2]{1,2,0:T(2,128)(2,1)S(1)}, u32[]{:S(2)}, u32[]{:S(2)}) async-start(bf16[32,2,2]{1,2,0:T(2,128)(2,1)} %copy.112), calls=%async_computation | async-start | bytes 32768 | tf_op jit(solution)/shard_map/all_to_all | solution.py:67
  25.7 10.4 %all-to-all-start.1 = ((bf16[32,16,2]{0,2,1:T(2,128)(2,1)}), bf16[32,16,2]{0,2,1:T(2,128)(2,1)S(1)}, u32[]{:S(2)}, u32[]{:S(2)}) async-start(bf16[32,16,2]{0,2,1:T(2,128)(2,1)} %bitcast), calls=%async_computation.1 | async-start | bytes 16384 | tf_op jit(solution)/shard_map/all_to_all | solution.py:80
  36.1 26.4 %all-to-all-start.2 = ((bf16[32,2,2,2048]{3,2,1,0:T(2,128)(2,1)}), bf16[32,2,2,2048]{3,2,1,0:T(2,128)(2,1)S(1)}, u32[]{:S(2)}, u32[]{:S(2)}) async-start(bf16[32,2,2,2048]{3,2,1,0:T(2,128)(2,1)} %reshape.68), calls=%async_computation.2 | async-start | bytes 1048576 | tf_op jit(solution)/shard_map/all_to_all | solution.py:66
  62.6 24.4 %all-to-all-start.4 = ((bf16[32,2,2,2048]{3,2,1,0:T(2,128)(2,1)}), bf16[32,2,2,2048]{3,2,1,0:T(2,128)(2,1)S(1)}, u32[]{:S(2)}, u32[]{:S(2)}) async-start(bf16[32,2,2,2048]{3,2,1,0:T(2,128)(2,1)} %reshape.71), calls=%async_computation.4 | async-start | bytes 1048576 | tf_op jit(solution)/shard_map/all_to_all | solution.py:65
  92.5 68.8 %all-to-all-start.3 = ((bf16[32,16,2,2048]{3,2,0,1:T(2,128)(2,1)}), bf16[32,16,2,2048]{3,2,0,1:T(2,128)(2,1)}, u32[]{:S(2)}, u32[]{:S(2)}) async-start(bf16[32,16,2,2048]{3,2,0,1:T(2,128)(2,1)} %bitcast.112), calls=%async_computation.3 | async-start | bytes 8388608 | tf_op jit(solution)/shard_map/all_to_all | solution.py:79
  161.3 67.2 %all-to-all-start.5 = ((bf16[16,32,1,2,2048]{4,3,1,2,0:T(2,128)(2,1)}), bf16[16,32,1,2,2048]{4,3,1,2,0:T(2,128)(2,1)}, u32[]{:S(2)}, u32[]{:S(2)}) async-start(bf16[16,32,1,2,2048]{4,3,1,2,0:T(2,128)(2,1)} %fusion.4), calls=%async_computation.5 | async-start | bytes 8388608 | tf_op jit(solution)/shard_map/all_to_all | solution.py:74
  237.2 11.4 %copy-start.6 = (bf16[2048,128]{1,0:T(8,128)(2,1)S(1)}, bf16[2048,128]{1,0:T(8,128)(2,1)}, u32[]{:S(2)}) copy-start(bf16[2048,128]{1,0:T(8,128)(2,1)} %param.14) | copy-start | bytes 1572868
  244.7 3.9 copy-start.1
  244.7 5.4 %copy-start.4 = (bf16[1024,2048]{1,0:T(8,128)(2,1)S(1)}, bf16[1024,2048]{1,0:T(8,128)(2,1)}, u32[]{:S(2)}) copy-start(bf16[1024,2048]{1,0:T(8,128)(2,1)} %reshape.70) | copy-start | bytes 12582916
  244.7 5.4 %copy-start.7 = (bf16[128,2048]{1,0:T(8,128)(2,1)S(1)}, bf16[128,2048]{1,0:T(8,128)(2,1)}, u32[]{:S(2)}) copy-start(bf16[128,2048]{1,0:T(8,128)(2,1)} %param.15) | copy-start | bytes 1572868
  272.1 108.9 %all-to-all-start.6 = ((bf16[32,16,2,2048]{3,2,0,1:T(2,128)(2,1)}), bf16[32,16,2,2048]{3,2,0,1:T(2,128)(2,1)}, u32[]{:S(2)}, u32[]{:S(2)}) async-start(bf16[32,16,2,2048]{3,2,0,1:T(2,128)(2,1)} %copy.120), calls=%async_computation.6 | async-start | bytes 8388608 | tf_op jit(solution)/shard_map/all_to_all | solution.py:92
  380.9 14.9 %all-to-all-start.8 = ((f32[32,2,2]{2,1,0:T(2,128)}), f32[32,2,2]{2,1,0:T(2,128)S(1)}, u32[]{:S(2)}, u32[]{:S(2)}) async-start(f32[32,2,2]{2,1,0:T(2,128)} %copy.123), calls=%async_computation.8 | async-start | bytes 65536 | tf_op jit(solution)/shard_map/all_to_all | solution.py:107
  395.8 50.7 %all-to-all-start.7 = ((f32[32,2,2,2048]{3,2,1,0:T(2,128)}), f32[32,2,2,2048]{3,2,1,0:T(2,128)S(1)}, u32[]{:S(2)}, u32[]{:S(2)}) async-start(f32[32,2,2,2048]{3,2,1,0:T(2,128)} %copy.121), calls=%async_computation.7 | async-start | bytes 2097152 | tf_op jit(solution)/shard_map/all_to_all | solution.py:106
  406.6 4.5 copy-start.2
  406.6 6.6 %copy-start.5 = (bf16[1024,2048]{1,0:T(8,128)(2,1)S(1)}, bf16[1024,2048]{1,0:T(8,128)(2,1)}, u32[]{:S(2)}) copy-start(bf16[1024,2048]{1,0:T(8,128)(2,1)} %reshape.70) | copy-start | bytes 12582916
